TPU v7x, 256 devices: a whole 4x4x8 slice. The times are simulated.
256 devices in a mesh: coil: 8 (over z_hi, x), ro: 32 (over y, z_lo, core).
Axes of the slice: x: 4, y: 4, z: 8 (z_hi: 2, z_lo: 4; z = z_hi * 4 + z_lo), core: 2. Of those that a mesh axis runs over, the one named last changes fastest.
Arguments:
- kspace: bfloat16 [2, 64, 32, 448, 320], P(None, 'coil', None, 'ro'), may hold values from -884272563206990856199 to 884272563206990856199
- sensitivity: bfloat16 [2, 64, 32, 448, 320], P(None, 'coil', 'ro'), may hold values from -0.75 to 0.75
- sampled: int32 [32, 448], replicated, may hold values 0 or 1
- pole_y: int32 [32, 320], replicated, may hold values from 4 to 112
- order_y: int32 [32, 320], replicated, may hold values from 1 to 3
- pole_z: int32 [32, 448], replicated, may hold values from 4 to 80
- order_z: int32 [32, 448], replicated, may hold values from 1 to 3
Outputs:
- image: float32 [2, 32, 448, 320], P(None, 'ro', 'coil')
All inputs are finite; a program needn't handle non-finite values.
Results may differ from a plain program's by a relative error of at most 0.0056.
Values may be sent and summed in bfloat16 or wider, within the bound.
A program may use at most 128 MiB of HBM per device.

v0:
```python
import math
import jax
import jax.numpy as jnp
from jax import lax
from jax.sharding import PartitionSpec as P


def dft_tables(length):
    index = jnp.arange(length, dtype=jnp.int32)
    product = index[:, None] * index[None, :] % length
    angle = product.astype(jnp.float32) * (2.0 * math.pi / length)
    factor = 1.0 / math.sqrt(length)
    return (
        (jnp.cos(angle) * factor).astype(jnp.bfloat16),
        (jnp.sin(angle) * factor).astype(jnp.bfloat16),
    )


def line_window(frequency, pole, degree):
    quotient = frequency / pole.astype(jnp.float32)
    return 1.0 / (1.0 + jnp.power(quotient, 2.0 * degree.astype(jnp.float32)))


def kz_transform(filtered, kz_cosine, kz_sine):
    real_part, imag_part = (filtered[0], filtered[1])
    hyb_real = jnp.einsum(
        "cakz,zn->cakn", real_part, kz_cosine, preferred_element_type=jnp.float32
    ) - jnp.einsum("cakz,zn->cakn", imag_part, kz_sine, preferred_element_type=jnp.float32)
    hyb_imag = jnp.einsum(
        "cakz,zn->cakn", real_part, kz_sine, preferred_element_type=jnp.float32
    ) + jnp.einsum("cakz,zn->cakn", imag_part, kz_cosine, preferred_element_type=jnp.float32)
    return jnp.stack([hyb_real, hyb_imag]).astype(jnp.bfloat16)


def on_device(kspace, sensitivity, sampled, pole_y, order_y, pole_z, order_z):
    lines_local = kspace.shape[3]
    kz_count = kspace.shape[4]
    ky_count = lines_local * lax.axis_size("ro")
    first_line = lax.axis_index("ro") * lines_local
    kz_cosine, kz_sine = dft_tables(kz_count)
    ky_cosine, ky_sine = dft_tables(ky_count)
    line_index = first_line + jnp.arange(lines_local, dtype=jnp.int32)
    freq_y = jnp.minimum(line_index, ky_count - line_index).astype(jnp.float32)
    col_index = jnp.arange(kz_count, dtype=jnp.int32)
    freq_z = jnp.minimum(col_index, kz_count - col_index).astype(jnp.float32)
    local_sampled = lax.dynamic_slice_in_dim(sampled, first_line, lines_local, 1)
    local_pole_z = lax.dynamic_slice_in_dim(pole_z, first_line, lines_local, 1)
    local_order_z = lax.dynamic_slice_in_dim(order_z, first_line, lines_local, 1)
    weight_y = local_sampled[:, :, None].astype(jnp.float32) * line_window(
        freq_y[None, :, None], pole_y[:, None, :], order_y[:, None, :]
    )
    weight_z = line_window(
        freq_z[None, None, :], local_pole_z[:, :, None], local_order_z[:, :, None]
    )
    filtered = (kspace.astype(jnp.float32) * (weight_y * weight_z)).astype(jnp.bfloat16)
    hybrid = kz_transform(filtered, kz_cosine, kz_sine)
    moved = lax.all_to_all(hybrid, "ro", split_axis=2, concat_axis=3, tiled=True)
    hyb_real, hyb_imag = (moved[0], moved[1])
    img_real = jnp.einsum(
        "nk,cakz->canz", ky_cosine, hyb_real, preferred_element_type=jnp.float32
    ) - jnp.einsum("nk,cakz->canz", ky_sine, hyb_imag, preferred_element_type=jnp.float32)
    img_imag = jnp.einsum(
        "nk,cakz->canz", ky_sine, hyb_real, preferred_element_type=jnp.float32
    ) + jnp.einsum("nk,cakz->canz", ky_cosine, hyb_imag, preferred_element_type=jnp.float32)
    map_real = sensitivity[0]
    map_imag = sensitivity[1]
    out_real = jnp.sum(map_real * img_real + map_imag * img_imag, axis=0)
    out_imag = jnp.sum(map_real * img_imag - map_imag * img_real, axis=0)
    partial_image = jnp.stack([out_real, out_imag])
    return lax.psum_scatter(partial_image, "coil", scatter_dimension=2, tiled=True)


def solution(mesh):
    return jax.shard_map(
        on_device,
        mesh=mesh,
        in_specs=(
            P(None, "coil", None, "ro", None),
            P(None, "coil", "ro", None, None),
            P(),
            P(),
            P(),
            P(),
            P(),
        ),
        out_specs=P(None, "ro", "coil", None),
        check_vma=False,
    )
```

profile of v0, /device:TPU:8, one launch (start us, length us, event | category | flops | bytes accessed | tf_op | source)
XLA Modules:
  0.0 342.3 jit_solution(6022209747926040694)
XLA Ops:
  6.6 0.9 constant_dynamic-slice_fusion
  7.4 0.1 copy.64
  7.5 0.1 copy.65
  7.6 0.1 constant_dynamic-slice_fusion.2
  7.7 0.1 copy.63
  7.8 0.8 convert_element_type.114
  8.6 0.8 convert_multiply_fusion.4
  9.4 2.3 fusion.15
  11.7 3.8 %multiply_convert_fusion = bf16[2,8,32,14,320]{4,2,3,1,0:T(8,128)(2,1)S(1)} fusion(bf16[2,8,32,14,320]{4,2,3,1,0:T(8,128)(2,1)} %param.7, f32[32,14,320]{2,0,1:T(8,128)S(1)} %fusion.15), kind=kLoop, calls=%fused_computation | loop fusion | flops 6881280 | bytes 9748480 | tf_op jit(solution)/shard_map/convert_element_type | solution.py:55
  15.5 3.4 fusion.7
  18.9 3.4 fusion.6
  22.3 3.8 %fusion.4 = bf16[1,8,32,14,320]{4,2,3,1,0:T(8,128)(2,1)S(1)} fusion(f32[8,32,14,320]{3,1,2,0:T(8,128)S(1)} %fusion.7, bf16[2,8,32,14,320]{4,2,3,1,0:T(8,128)(2,1)S(1)} %multiply_convert_fusion), kind=kOutput, calls=%fused_computation.12 | convolution fusion | flops 737423360 | bytes 10551296 | tf_op jit(solution)/shard_map/cakz,zn->cakn/dot_general | solution.py:28
  26.1 3.6 %fusion.5 = bf16[1,8,32,14,320]{4,2,3,1,0:T(8,128)(2,1)S(1)} fusion(f32[8,32,14,320]{3,1,2,0:T(8,128)S(1)} %fusion.6, bf16[2,8,32,14,320]{4,2,3,1,0:T(8,128)(2,1)S(1)} %multiply_convert_fusion), kind=kOutput, calls=%fused_computation.13 | convolution fusion | flops 737423360 | bytes 10551296 | tf_op jit(solution)/shard_map/cakz,zn->cakn/dot_general | solution.py:31
  29.7 1.1 pad_maximum_fusion
  30.8 3.3 copy.53
  34.1 130.9 %all_to_all.4 = bf16[2,8,32,14,320]{4,1,3,0,2:T(8,128)(2,1)S(1)} all-to-all(bf16[2,8,32,14,320]{4,1,3,0,2:T(8,128)(2,1)S(1)} %copy.53), channel_id=1, replica_groups=mesh['coil'=8,'ro'=32] {'ro'}, dimensions={2} | all-to-all | bytes 9175040 | tf_op jit(solution)/shard_map/all_to_all | solution.py:57
  165.0 3.1 fusion.72
  168.1 3.7 %copy.54 = bf16[8,448,320]{1,2,0:T(8,128)(2,1)S(1)} copy(bf16[8,448,320]{2,0,1:T(8,128)(2,1)} %bitcast.70) | data formatting | bytes 4587520 | tf_op jit(solution)/shard_map/reshape.4
  171.8 8.5 %fusion.26 = f32[8,320,448]{2,1,0:T(8,128)} fusion(bf16[8,448,320]{1,2,0:T(8,128)(2,1)S(1)} %copy.54), kind=kOutput, calls=%fused_computation.51 | convolution fusion | flops 1029812224 | bytes 6881280 | tf_op jit(solution)/shard_map/nk,cakz->canz/dot_general | solution.py:62
  180.4 8.5 %fusion.30 = f32[8,320,448]{2,1,0:T(8,128)} fusion(bf16[8,448,320]{1,2,0:T(8,128)(2,1)S(1)} %copy.54), kind=kOutput, calls=%fused_computation.52 | convolution fusion | flops 1029812224 | bytes 6881280 | tf_op jit(solution)/shard_map/nk,cakz->canz/dot_general | solution.py:59
  188.9 3.7 %copy.55 = bf16[8,448,320]{1,2,0:T(8,128)(2,1)S(1)} copy(bf16[8,448,320]{2,0,1:T(8,128)(2,1)} %bitcast.69) | data formatting | bytes 4587520 | tf_op jit(solution)/shard_map/reshape.9
  192.6 8.8 %convolution_add_fusion = f32[8,320,448]{2,1,0:T(8,128)S(1)} fusion(f32[8,320,448]{2,1,0:T(8,128)} %fusion.26, bf16[8,448,320]{1,2,0:T(8,128)(2,1)S(1)} %copy.55), kind=kOutput, calls=%fused_computation.20 | convolution fusion | flops 1030959104 | bytes 11468800 | tf_op jit(solution)/shard_map/nk,cakz->canz/dot_general | solution.py:64
  201.5 0.0 copy-start.1
  201.5 9.9 %fusion.1 = (f32[448,320]{0,1:T(8,128)S(1)}, f32[448,320]{0,1:T(8,128)S(1)}) fusion(f32[8,320,448]{2,1,0:T(8,128)S(1)} %convolution_add_fusion, bf16[2,8,1,448,320]{3,4,1,2,0:T(8,128)(2,1)} %bitcast.73, f32[8,320,448]{2,1,0:T(8,128)S(1)} %copy-done.2, bf16[8,448,320]{1,2,0:T(8,128)(2,1)S(1)} %copy.55), kind=kOutput, calls=%fused_computation.9 | convolution fusion | flops 1042141184 | bytes 17203200 | tf_op jit(solution)/shard_map/nk,cakz->canz/dot_general | solution.py:61
  211.4 0.0 copy-start.3
  211.4 0.1 pad_maximum_fusion.1
  211.5 2.2 copy.59
  213.6 0.0 all-reduce.3.cloned.1.call-update
  213.7 0.6 dynamic-slice
  214.9 118.9 %all-reduce.3.cloned.1.call-done = f32[2,1,448,320]{3,0,1,2:T(2,128)} async-done(((f32[2,1,448,320]{3,0,1,2:T(2,128)}), f32[2,1,448,320]{3,0,1,2:T(2,128)}) %all-reduce.3.cloned.1.call-update) | async-done | bytes 1146896
  333.9 1.0 constant_dynamic-slice_fusion.3
  334.8 0.7 copy.60
  (12 shorter events, 0.0 us)
Async XLA Ops:
  6.5 1.1 copy-start
  6.5 327.3 %all-reduce.3.cloned.1.call-start = ((), (), s32[]{:S(2)}) async-start(), calls=%async_computation.1 | async-start | bytes 2752512
  192.6 8.9 %copy-start.2 = (f32[8,320,448]{2,1,0:T(8,128)S(1)}, f32[8,320,448]{2,1,0:T(8,128)}, u32[]{:S(2)}) copy-start(f32[8,320,448]{2,1,0:T(8,128)} %fusion.30) | copy-start | bytes 13762564
  201.5 134.0 %copy-start.1 = (s32[32,448]{1,0:T(8,128)S(1)}, s32[32,448]{1,0:T(8,128)}, u32[]{:S(2)}) copy-start(s32[32,448]{1,0:T(8,128)} %param.9) | copy-start | bytes 172036
  211.4 2.3 copy-start.3
Sparse Core Ops, SparseCore 0:
  213.8 120.0 all-reduce.2
where the time goes:
time: 343 us; the launch traced here: 342 us
  blocking collectives  131 us (38%)
  waiting for transfers between devices  119 us (35%)
  matrix products  50.1 us (15%)
  local copies, waits for them, and re-layouts  19.3 us (6%)
  between operations  14.2 us (4%)
  other arithmetic  8.9 us (3%)
    all_to_all x1, blocking collectives, on_device(): lax.all_to_all(hybrid, 'ro', split_axis=2, concat_axis=3, tiled=True)  131 us
    unnamed x2, waiting for transfers between devices  119 us
    dot_general x1, matrix products, on_device(): jnp.einsum('nk,cakz->canz', ky_sine, hyb_imag, preferred_element_type=jnp...  9.9 us
    dot_general x1, matrix products, on_device(): jnp.einsum('nk,cakz->canz', ky_cosine, hyb_imag, preferred_element_type=j...  8.83 us
    dot_general x1, matrix products, on_device(): jnp.einsum('nk,cakz->canz', ky_sine, hyb_real, preferred_element_type=jnp...  8.54 us
    dot_general x1, matrix products, on_device(): jnp.einsum('nk,cakz->canz', ky_cosine, hyb_real, preferred_element_type=j...  8.53 us
    another operation x2, local copies, waits for them, and re-layouts  7.41 us
  transfers between devices with their start and end apart: 1, of which 1 were waited for; matrix products, arithmetic and copies ran while one was open for 0% of the time, Pallas kernels for 0%

commit v1 on v0

--- a/solution.py
+++ b/solution.py
@@ -54,7 +54,10 @@
     )
     filtered = (kspace.astype(jnp.float32) * (weight_y * weight_z)).astype(jnp.bfloat16)
     hybrid = kz_transform(filtered, kz_cosine, kz_sine)
-    moved = lax.all_to_all(hybrid, "ro", split_axis=2, concat_axis=3, tiled=True)
+    moved = jnp.concatenate(
+        lax.all_to_all(jnp.stack(jnp.split(hybrid, lax.axis_size("ro"), axis=2)), "ro", 0, 0),
+        axis=3,
+    )
     hyb_real, hyb_imag = (moved[0], moved[1])
     img_real = jnp.einsum(
         "nk,cakz->canz", ky_cosine, hyb_real, preferred_element_type=jnp.float32

time: 343 us -> 326 us (0.950)
  waiting for transfers between devices: 119 us -> 88.2 us
  other arithmetic: 8.9 us -> 23.3 us
    unnamed x2 -> x1, waiting for transfers between devices: 119 us -> 0.02 us
    reduce_scatter x0 -> x1, waiting for transfers between devices: none -> 88.2 us  [on_device(): lax.psum_scatter(partial_image, 'coil', scatter_dimension=2, tiled=True)]
    another operation x1 -> x4, other arithmetic: 1.1 us -> 14.5 us  [kz_transform(): return jnp.stack([hyb_real, hyb_imag]).astype(jnp.bfloat16)]
    another operation x4, local copies, waits for them, and re-layouts: 12.9 us -> 9.14 us
where the time goes in v1:
time: 326 us; the launch traced here: 325 us
  blocking collectives  131 us (40%)
  waiting for transfers between devices  88.2 us (27%)
  matrix products  50.9 us (16%)
  other arithmetic  23.3 us (7%)
  local copies, waits for them, and re-layouts  17.8 us (5%)
  between operations  14 us (4%)
    all_to_all x1, blocking collectives, on_device(): lax.all_to_all(jnp.stack(jnp.split(hybrid, lax.axis_size('ro'), axis=2)),...  131 us
    reduce_scatter x1, waiting for transfers between devices, on_device(): lax.psum_scatter(partial_image, 'coil', scatter_dimension=2, tiled=True)  88.2 us
    another operation x4, other arithmetic, kz_transform(): return jnp.stack([hyb_real, hyb_imag]).astype(jnp.bfloat16)  14.5 us
    dot_general x1, matrix products, on_device(): jnp.einsum('nk,cakz->canz', ky_sine, hyb_imag, preferred_element_type=jnp...  10.7 us
    dot_general x1, matrix products, on_device(): jnp.einsum('nk,cakz->canz', ky_cosine, hyb_imag, preferred_element_type=j...  8.83 us
    dot_general x1, matrix products, on_device(): jnp.einsum('nk,cakz->canz', ky_sine, hyb_real, preferred_element_type=jnp...  8.54 us
    dot_general x1, matrix products, on_device(): jnp.einsum('nk,cakz->canz', ky_cosine, hyb_real, preferred_element_type=j...  8.54 us
    another operation x2, local copies, waits for them, and re-layouts  7.41 us
  transfers between devices with their start and end apart: 1, of which 1 were waited for; matrix products, arithmetic and copies ran while one was open for 0% of the time, Pallas kernels for 0%

profile of v1, /device:TPU:8, one launch (start us, length us, event | category | flops | bytes accessed | tf_op | source)
XLA Modules:
  0.0 325.1 jit_solution(13415171226506324630)
XLA Ops:
  6.6 0.8 copy-done
  7.4 0.1 constant_dynamic-slice_fusion.2
  7.5 0.1 copy.1987
  7.5 0.9 constant_dynamic-slice_fusion
  8.4 0.1 copy.1989
  8.5 0.1 copy.1988
  8.6 0.8 convert_element_type.114
  9.4 0.8 convert_multiply_fusion.4
  10.2 2.3 fusion.15
  12.5 3.8 %multiply_convert_fusion = bf16[2,8,32,14,320]{4,2,3,1,0:T(8,128)(2,1)S(1)} fusion(bf16[2,8,32,14,320]{4,2,3,1,0:T(8,128)(2,1)} %param.7, f32[32,14,320]{2,0,1:T(8,128)S(1)} %fusion.15), kind=kLoop, calls=%fused_computation.62 | loop fusion | flops 6881280 | bytes 9748480 | tf_op jit(solution)/shard_map/convert_element_type | solution.py:55
  16.2 3.4 %fusion.6 = f32[8,32,14,320]{3,1,2,0:T(8,128)S(1)} fusion(bf16[2,8,32,14,320]{4,2,3,1,0:T(8,128)(2,1)S(1)} %multiply_convert_fusion), kind=kOutput, calls=%fused_computation.77 | convolution fusion | flops 735129600 | bytes 7340032 | tf_op jit(solution)/shard_map/cakz,zn->cakn/dot_general | solution.py:29
  19.7 3.4 %fusion.7 = f32[8,32,14,320]{3,1,2,0:T(8,128)S(1)} fusion(bf16[2,8,32,14,320]{4,2,3,1,0:T(8,128)(2,1)S(1)} %multiply_convert_fusion), kind=kOutput, calls=%fused_computation.78 | convolution fusion | flops 735129600 | bytes 7340032 | tf_op jit(solution)/shard_map/cakz,zn->cakn/dot_general | solution.py:26
  23.1 3.8 %fusion.5 = bf16[1,8,32,14,320]{4,2,3,1,0:T(8,128)(2,1)S(1)} fusion(f32[8,32,14,320]{3,1,2,0:T(8,128)S(1)} %fusion.6, bf16[2,8,32,14,320]{4,2,3,1,0:T(8,128)(2,1)S(1)} %multiply_convert_fusion), kind=kOutput, calls=%fused_computation.74 | convolution fusion | flops 737423360 | bytes 10551296 | tf_op jit(solution)/shard_map/cakz,zn->cakn/dot_general | solution.py:31
  26.9 3.6 %fusion.4 = bf16[1,8,32,14,320]{4,2,3,1,0:T(8,128)(2,1)S(1)} fusion(f32[8,32,14,320]{3,1,2,0:T(8,128)S(1)} %fusion.7, bf16[2,8,32,14,320]{4,2,3,1,0:T(8,128)(2,1)S(1)} %multiply_convert_fusion), kind=kOutput, calls=%fused_computation.73 | convolution fusion | flops 737423360 | bytes 10551296 | tf_op jit(solution)/shard_map/cakz,zn->cakn/dot_general | solution.py:28
  30.5 2.4 fusion.61
  32.9 4.3 %fusion.62 = (bf16[2,8,1,14,320]{4,2,3,1,0:T(2,128)(2,1)S(1)}, bf16[2,8,1,14,320]{4,2,3,1,0:T(2,128)(2,1)S(1)}, bf16[2,8,1,14,320]{4,2,3,1,0:T(2,128)(2,1)S(1)},...) fusion(bf16[1,8,32,14,320]{4,2,3,1,0:T(8,128)(2,1)S(1)} %fusion, ...), kind=kLoop, calls=%fused_computation.142 | loop fusion | flops 645120 | bytes 5877760 | tf_op jit(solution)/shard_map/stack | solution.py:32
  37.2 3.5 %pad_maximum_fusion.1 = (bf16[2,8,1,14,320]{4,2,3,1,0:T(2,128)(2,1)S(1)}, bf16[2,8,1,14,320]{4,2,3,1,0:T(2,128)(2,1)S(1)}, bf16[2,8,1,14,320]{4,2,3,1,0:T(2,128)...) fusion(bf16[1,8,32,14,320]{4,2,3,1,0:T(8,128)(2,1)S(1)} %fusion, ...), kind=kLoop, calls=%fused_computation.143 | loop fusion | flops 2580480 | bytes 5877760 | tf_op jit(solution)/shard_map/stack | solution.py:32
  40.7 4.3 %fusion.32 = (bf16[2,8,1,14,320]{4,2,3,1,0:T(2,128)(2,1)S(1)}, bf16[2,8,1,14,320]{4,2,3,1,0:T(2,128)(2,1)S(1)}, bf16[2,8,1,14,320]{4,2,3,1,0:T(2,128)(2,1)S(1)},...) fusion(bf16[1,8,32,14,320]{4,2,3,1,0:T(8,128)(2,1)S(1)} %fusion, ...), kind=kLoop, calls=%fused_computation.112 | loop fusion | flops 645120 | bytes 5877760 | tf_op jit(solution)/shard_map/stack | solution.py:32
  47.5 1.7 copy.1977
  49.2 130.9 %all_to_all.5 = bf16[32,2,8,1,14,320]{5,2,4,3,1,0:T(8,128)(2,1)S(1)} all-to-all(bf16[32,2,8,1,14,320]{5,2,4,3,1,0:T(8,128)(2,1)S(1)} %copy.1977), channel_id=1, replica_groups=mesh['coil'=8,'ro'=32] {'ro'}, dimensions={0} | all-to-all | bytes 9175040 | tf_op jit(solution)/shard_map/all_to_all | solution.py:58
  180.1 3.1 fusion.103
  183.2 3.7 %copy.1978 = bf16[8,448,320]{1,2,0:T(8,128)(2,1)S(1)} copy(bf16[8,448,320]{2,0,1:T(8,128)(2,1)} %bitcast.158) | data formatting | bytes 4587520 | tf_op jit(solution)/shard_map/reshape.4
  186.9 8.5 %fusion.26 = f32[8,320,448]{2,1,0:T(8,128)} fusion(bf16[8,448,320]{1,2,0:T(8,128)(2,1)S(1)} %copy.1978), kind=kOutput, calls=%fused_computation.110 | convolution fusion | flops 1029812224 | bytes 6881280 | tf_op jit(solution)/shard_map/nk,cakz->canz/dot_general | solution.py:65
  195.4 8.5 %fusion.30 = f32[8,320,448]{2,1,0:T(8,128)} fusion(bf16[8,448,320]{1,2,0:T(8,128)(2,1)S(1)} %copy.1978), kind=kOutput, calls=%fused_computation.111 | convolution fusion | flops 1029812224 | bytes 6881280 | tf_op jit(solution)/shard_map/nk,cakz->canz/dot_general | solution.py:62
  204.0 3.7 %copy.1979 = bf16[8,448,320]{1,2,0:T(8,128)(2,1)S(1)} copy(bf16[8,448,320]{2,0,1:T(8,128)(2,1)} %bitcast.157) | data formatting | bytes 4587520 | tf_op jit(solution)/shard_map/reshape.8
  207.7 8.8 %convolution_add_fusion = f32[8,320,448]{2,1,0:T(8,128)S(1)} fusion(f32[8,320,448]{2,1,0:T(8,128)} %fusion.26, bf16[8,448,320]{1,2,0:T(8,128)(2,1)S(1)} %copy.1979), kind=kOutput, calls=%fused_computation.79 | convolution fusion | flops 1030959104 | bytes 11468800 | tf_op jit(solution)/shard_map/nk,cakz->canz/dot_general | solution.py:67
  216.6 10.7 %fusion.1 = (f32[448,320]{0,1:T(8,128)}, f32[448,320]{0,1:T(8,128)S(1)}) fusion(f32[8,320,448]{2,1,0:T(8,128)S(1)} %convolution_add_fusion, bf16[2,8,1,448,320]{3,4,2,1,0:T(8,128)(2,1)} %param.8, f32[8,320,448]{2,1,0:T(8,128)S(1)} %copy-done.2, bf16[8,448,320]{1,2,0:T(8,128)(2,1)S(1)} %copy.1979), kind=kOutput, calls=%fused_computation.70 | convolution fusion | flops 1042141184 | bytes 17203200 | tf_op jit(solution)/shard_map/nk,cakz->canz/dot_general | solution.py:64
  227.3 1.3 copy.1982
  228.6 0.2 copy.1983
  228.9 1.2 pad_maximum_fusion
  230.1 0.0 reduce-scatter.2.cloned.1.call-update
  230.1 88.2 %reduce-scatter.2.cloned.1.call-done = f32[2,1,56,320]{3,2,1,0:T(8,128)} async-done(((f32[2,1,448,320]{3,2,1,0:T(8,128)}), f32[2,1,56,320]{3,2,1,0:T(8,128)}) %reduce-scatter.2.cloned.1.call-update) | async-done | bytes 143376 | tf_op jit(solution)/shard_map/reduce_scatter | solution.py:73
  (74 shorter events, 2.1 us)
Async XLA Ops:
  6.5 0.8 copy-start
  6.5 311.7 %reduce-scatter.2.cloned.1.call-start = ((), (), s32[]{:S(2)}) async-start(), calls=%async_computation.2 | async-start | bytes 1548288 | tf_op jit(solution)/shard_map/reduce_scatter | solution.py:73
  207.7 8.9 %copy-start.2 = (f32[8,320,448]{2,1,0:T(8,128)S(1)}, f32[8,320,448]{2,1,0:T(8,128)}, u32[]{:S(2)}) copy-start(f32[8,320,448]{2,1,0:T(8,128)} %fusion.30) | copy-start | bytes 13762564
  216.5 101.7 %copy-start.1 = (s32[32,448]{1,0:T(8,128)S(1)}, s32[32,448]{1,0:T(8,128)}, u32[]{:S(2)}) copy-start(s32[32,448]{1,0:T(8,128)} %param.9) | copy-start | bytes 172036
Sparse Core Ops, SparseCore 0:
  230.2 87.9 reduce-scatter.1
